TPU v7x, 32 devices: a whole 2x2x4 slice. The times are simulated.
32 devices in a mesh: groups: 2 (over y), fsdp: 8 (over z, x), seq: 2 (over core).
Axes of the slice: x: 2, y: 2, z: 4, core: 2. Of those that a mesh axis runs over, the one named last changes fastest.
Arguments:
- tokens: bfloat16 [2048, 8192], P(('groups', 'fsdp', 'seq')), parts along dimension 0, may hold values from -6 to 6
- gate_blocks: bfloat16 [1280, 4096], P('fsdp'), may hold values from -0.09375 to 0.09375
- gate_slot: int32 [1280], P('fsdp'), may hold values from 0 to 256, as said below
- up_blocks: bfloat16 [1280, 4096], P('fsdp'), may hold values from -0.09375 to 0.09375
- up_slot: int32 [1280], P('fsdp'), may hold values from 0 to 256, as said below
- down_blocks: bfloat16 [1280, 4096], P('fsdp'), may hold values from -0.25 to 0.25
- down_slot: int32 [1280], P('fsdp'), may hold values from 0 to 256, as said below
- sketch: bfloat16 [32, 8192], P(None, 'fsdp'), may hold values from -0.0625 to 0.0625
- probe_index: int32 [16, 256], replicated, may hold values from 0 to 8191
- probe_value: float32 [16, 256], replicated, may hold values from -32 to 32
Outputs:
- products: float32 [32, 8192], P('groups', 'fsdp'), parts along dimension 0
There are 2 independent parts, one for each index of `groups`. A program takes and returns all parts, laid end to end along the dimension named above; an argument that names none is the same for every part. Nothing has to cross between parts.
Inputs may be any that keep to these rules, and one draw needn't show every extreme that they name: `gate_slot`: slots j * 160 to (j + 1) * 160 - 1 belong to fsdp owner j; they hold distinct block numbers below 256, filled slots first, then the value 256 for empty slots. Every owner fills 3 * 32 slots or more, and in every draw some owner fills all 160. `up_slot`: as for gate_slot, drawn independently. `down_slot`: as for gate_slot, drawn independently.
All inputs are finite; a program needn't handle non-finite values.
Results may differ from a plain program's by a relative error of at most 0.0038.
Values may be sent and summed in bfloat16 or wider, within the bound.
No kernel may reach another device: no remote copies, remote signals or barrier semaphores. Data moves between devices by JAX's collectives and lax.ppermute only.
A program may use at most 128 MiB of HBM per device.

v0:
```python
import jax
import jax.numpy as jnp
from jax import lax
from jax.sharding import PartitionSpec as P

HID_DEV = 128
BLK = 64
P_SIZE = 16
K = 32


def unpack(blocks, slot_ids, cell_total):
    holder = jnp.zeros((cell_total + 1, blocks.shape[1]), blocks.dtype)
    return holder.at[slot_ids].set(blocks)[:cell_total]


def contract_last(first_mat, second_mat):
    return lax.dot_general(
        first_mat, second_mat, (((1,), (1,)), ((), ())), preferred_element_type=jnp.float32
    )


def per_device(
    tokens,
    gate_blocks,
    gate_slot,
    up_blocks,
    up_slot,
    down_blocks,
    down_slot,
    sketch,
    probe_index,
    probe_value,
):
    owners = lax.axis_size("fsdp")
    model_width = tokens.shape[1]
    local_width = model_width // owners
    block_rows = local_width // BLK
    hidden = HID_DEV
    col_blocks = hidden * owners // BLK
    cell_total = block_rows * col_blocks
    gate_dense = unpack(gate_blocks, gate_slot, cell_total).reshape(
        block_rows, col_blocks, BLK, BLK
    )
    up_dense = unpack(up_blocks, up_slot, cell_total).reshape(block_rows, col_blocks, BLK, BLK)
    stacked = jnp.stack([gate_dense, up_dense], axis=1)
    stacked = stacked.reshape(block_rows, 2, owners, hidden // BLK, BLK, BLK)
    stacked = stacked.transpose(0, 4, 2, 1, 3, 5).reshape(local_width, owners * 2 * hidden)
    both_weights = lax.all_to_all(stacked, "fsdp", split_axis=1, concat_axis=0, tiled=True)
    picked = both_weights[probe_index].astype(jnp.float32)
    probe_both = jnp.sum(picked * probe_value[:, :, None], axis=1)
    preact = jnp.dot(
        lax.all_gather(tokens, "fsdp", axis=0, tiled=True),
        both_weights,
        preferred_element_type=jnp.float32,
    )
    row_count = preact.shape[0]
    gate_pre = preact[:, :hidden]
    up_pre = preact[:, hidden:]
    down_dense = unpack(down_blocks, down_slot, cell_total).reshape(
        col_blocks, block_rows, BLK, BLK
    )
    down_dense = down_dense.transpose(0, 2, 1, 3).reshape(col_blocks * BLK, local_width)
    down_rows = lax.all_to_all(down_dense, "fsdp", split_axis=0, concat_axis=1, tiled=True)
    full_sketch = lax.all_gather(sketch, "fsdp", axis=1, tiled=True)
    projected = contract_last(down_rows, full_sketch)
    projected = projected.astype(jnp.bfloat16)
    sigmoid_g = jax.nn.sigmoid(gate_pre)
    activated = gate_pre * sigmoid_g
    slope_g = sigmoid_g * (1.0 + gate_pre * (1.0 - sigmoid_g))
    lead_term = slope_g * up_pre
    tangent = (
        lead_term[:, None, :] * probe_both[None, :, :hidden]
        + activated[:, None, :] * probe_both[None, :, hidden:]
    )
    tangent = tangent.astype(jnp.bfloat16)
    partial_sketch = jnp.dot(
        tangent.reshape(row_count * P_SIZE, hidden), projected, preferred_element_type=jnp.float32
    )
    partial_sketch = partial_sketch.reshape(row_count, P_SIZE * K)
    sketch_rows = lax.psum(partial_sketch, "fsdp").astype(jnp.bfloat16)
    backward = contract_last(sketch_rows.reshape(row_count * P_SIZE, K), projected).reshape(
        row_count, P_SIZE, hidden
    )
    summed = jnp.concatenate(
        [
            jnp.sum(backward * lead_term[:, None, :], axis=0),
            jnp.sum(backward * activated[:, None, :], axis=0),
        ],
        axis=1,
    )
    summed = lax.psum(summed, "seq").astype(jnp.bfloat16)
    products = contract_last(summed, both_weights)
    return lax.psum_scatter(products, "fsdp", scatter_dimension=1, tiled=True)


def solution(mesh):
    in_specs = (
        P(("groups", "fsdp", "seq"), None),
        P("fsdp", None),
        P("fsdp"),
        P("fsdp", None),
        P("fsdp"),
        P("fsdp", None),
        P("fsdp"),
        P(None, "fsdp"),
        P(),
        P(),
    )
    out_specs = P("groups", "fsdp")
    return jax.shard_map(
        per_device, mesh=mesh, in_specs=in_specs, out_specs=out_specs, check_vma=False
    )
```

profile of v0, /device:TPU:0, one launch (start us, length us, event | category | flops | bytes accessed | tf_op | source)
XLA Modules:
  0.0 471.8 jit_solution(3671803869858965092)
XLA Ops:
  6.5 0.0 all-gather.2.cloned.1.call-start
  6.5 0.7 all-gather.2.cloned.1.call-update
  7.3 0.7 compare_select_fusion.1
  7.9 3.9 scatter_custom_fusion.2
  11.8 1.5 slice.36
  13.3 6.9 %reshape.39 = bf16[16,16,64,64]{3,2,1,0:T(8,128)(2,1)} reshape(bf16[256,4096]{1,0:T(8,128)(2,1)} %slice.36) | data formatting | bytes 4194304 | tf_op jit(solution)/shard_map/reshape | solution.py:60
  20.2 8.0 %copy.32 = bf16[16,16,64,64]{3,1,2,0:T(8,128)(2,1)} copy(bf16[16,16,64,64]{3,2,1,0:T(8,128)(2,1)} %reshape.39) | data formatting | bytes 4194304 | tf_op jit(solution)/shard_map/reshape | solution.py:60
  28.2 6.5 %all_to_all.32 = bf16[8,128,1024]{2,1,0:T(8,128)(2,1)} reshape(bf16[16,64,16,64]{3,2,1,0:T(8,128)(2,1)} %bitcast.42) | data formatting | bytes 4194304 | tf_op jit(solution)/shard_map/all_to_all | solution.py:64
  34.8 7.3 %all-to-all-start.1 = ((bf16[8,128,1024]{2,1,0:T(8,128)(2,1)}), bf16[8,128,1024]{2,1,0:T(8,128)(2,1)}, u32[]{:S(2)}, u32[]{:S(2)}) async-start(bf16[8,128,1024]{2,1,0:T(8,128)(2,1)} %all_to_all.32), calls=%async_computation.1 | async-start | bytes 4194304 | tf_op jit(solution)/shard_map/all_to_all | solution.py:64
  42.0 0.0 copy-done.3
  42.0 4.0 scatter_custom_fusion
  46.1 1.5 slice.30
  47.6 6.9 %stack.7 = bf16[16,1,8,2,64,64]{5,4,3,2,0,1:T(8,128)(2,1)} reshape(bf16[256,4096]{1,0:T(8,128)(2,1)} %slice.30) | data formatting | bytes 4194304 | tf_op jit(solution)/shard_map/stack | solution.py:46
  54.5 0.0 copy-done.4
  54.5 3.9 scatter_custom_fusion.1
  58.3 1.5 slice.31
  59.9 6.9 %stack.8 = bf16[16,1,8,2,64,64]{5,4,3,2,0,1:T(8,128)(2,1)} reshape(bf16[256,4096]{1,0:T(8,128)(2,1)} %slice.31) | data formatting | bytes 4194304 | tf_op jit(solution)/shard_map/stack | solution.py:46
  66.7 8.6 %maximum_bitcast_fusion = bf16[16,64,8,2,2,64]{5,1,4,2,0,3:T(8,128)(2,1)} fusion(bf16[16,1,8,2,64,64]{5,4,3,2,0,1:T(8,128)(2,1)} %stack.8, bf16[16,1,8,2,64,64]{5,4,3,2,0,1:T(8,128)(2,1)} %stack.7), kind=kLoop, calls=%fused_computation.4 | loop fusion | flops 2097152 | bytes 8388608 | tf_op jit(solution)/shard_map/transpose | solution.py:48
  75.3 13.1 %copy.20 = bf16[16,64,8,2,2,64]{1,0,5,4,3,2:T(8,128)(2,1)} copy(bf16[16,64,8,2,2,64]{5,1,4,2,0,3:T(8,128)(2,1)} %maximum_bitcast_fusion) | data formatting | bytes 8388608 | tf_op jit(solution)/shard_map/transpose | solution.py:48
  88.4 12.0 %all_to_all.28 = bf16[1024,8,256]{0,2,1:T(8,128)(2,1)} reshape(bf16[16,64,8,2,2,64]{1,0,5,4,3,2:T(8,128)(2,1)} %copy.20) | data formatting | bytes 8388608 | tf_op jit(solution)/shard_map/all_to_all | solution.py:49
  100.4 34.2 %all-to-all-done.1 = bf16[8,128,1024]{2,1,0:T(8,128)(2,1)} async-done(((bf16[8,128,1024]{2,1,0:T(8,128)(2,1)}), bf16[8,128,1024]{2,1,0:T(8,128)(2,1)}, u32[]{:S(2)}, u32[]{:S(2)}) %all-to-all-start.1) | async-done | bytes 2097184 | tf_op jit(solution)/shard_map/all_to_all | solution.py:64
  134.5 5.9 %all-to-all-start = ((bf16[1024,8,256]{0,2,1:T(8,128)(2,1)}), bf16[1024,8,256]{0,2,1:T(8,128)(2,1)}, u32[]{:S(2)}, u32[]{:S(2)}) async-start(bf16[1024,8,256]{0,2,1:T(8,128)(2,1)} %all_to_all.28), calls=%async_computation | async-start | bytes 8388608 | tf_op jit(solution)/shard_map/all_to_all | solution.py:49
  140.4 0.0 reduce-scatter.2.cloned.1.call-start
  140.5 0.0 copy-done.2
  140.5 141.7 %all_gather.7 = bf16[32,8192]{1,0:T(8,128)(2,1)S(1)} all-gather(bf16[32,1024]{1,0:T(8,128)(2,1)S(1)} %copy-done), channel_id=1, replica_groups=mesh['groups'=2,'fsdp'=8,'seq'=2] {'fsdp'}, dimensions={1}, use_global_device_ids=true | all-gather | bytes 589824 | tf_op jit(solution)/shard_map/all_gather | solution.py:65
  282.2 3.0 copy.26
  285.3 0.4 convolution_convert_fusion
  285.7 0.0 all-to-all-done
  285.7 6.5 %copy.21 = bf16[8,1024,256]{2,1,0:T(8,128)(2,1)} copy(bf16[8,1024,256]{1,2,0:T(8,128)(2,1)} %bitcast.1) | data formatting | bytes 8388608 | tf_op jit(solution)/shard_map/all_to_all | solution.py:49
  292.2 15.7 %gather_fusion = bf16[4096,256]{1,0:T(8,128)(2,1)S(1)} fusion(bf16[8192,256]{1,0:T(8,128)(2,1)} %bitcast.39, s32[4096]{0:T(1024)S(1)} %broadcast_clamp_fusion), kind=kCustom, calls=%fused_computation | custom fusion | bytes 4210688 | tf_op jit(solution)/shard_map/gather | solution.py:50
  307.9 0.0 copy-done.1
  308.0 0.7 fusion
  308.7 0.0 all-gather.2.cloned.1.call-done
  308.7 7.0 %convolution_bitcast_fusion = f32[512,256]{0,1:T(8,128)S(1)} fusion(bf16[8192,256]{1,0:T(8,128)(2,1)} %bitcast.40, bf16[512,8192]{1,0:T(8,128)(2,1)} %all-gather.2.cloned.1.call-done), kind=kOutput, calls=%fused_computation.11 | convolution fusion | flops 2147483648 | bytes 13107200 | tf_op jit(solution)/shard_map/dot_general | solution.py:52
  315.8 0.1 slice_multiply_fusion
  315.9 0.1 copy.22
  316.0 0.1 copy.23
  316.2 0.5 add_convert_fusion
  316.7 1.4 copy.24
  318.1 2.6 fusion.14
  320.7 3.5 reshape.40
  324.2 70.7 %all-reduce.1 = bf16[512,512]{1,0:T(8,128)(2,1)S(1)} all-reduce(f32[512,512]{1,0:T(8,128)S(1)} %reshape.40), channel_id=1, replica_groups=mesh['groups'=2,'fsdp'=8,'seq'=2] {'fsdp'}, use_global_device_ids=true, to_apply=%region_4.0 | all-reduce | flops 262144 | bytes 1572864 | tf_op jit(solution)/shard_map/psum | solution.py:81
  395.0 0.2 copy.28
  395.2 1.0 multiply_reduce_fusion.1
  396.2 3.4 psum.15
  399.6 4.2 fusion.15
  403.7 0.0 reduce-scatter.2.cloned.1.call-update
  403.8 61.1 %reduce-scatter.2.cloned.1.call-done = f32[16,1024]{1,0:T(8,128)} async-done(((f32[16,8192]{1,0:T(8,128)}), f32[16,1024]{1,0:T(8,128)}) %reduce-scatter.2.cloned.1.call-update) | async-done | bytes 65552 | tf_op jit(solution)/shard_map/reduce_scatter | solution.py:94
  (13 shorter events, 0.0 us)
Async XLA Ops:
  6.5 302.2 %all-gather.2.cloned.1.call-start = ((), (), s32[]{:S(2)}) async-start(), calls=%async_computation.3 | async-start | bytes 9437184 | tf_op jit(solution)/shard_map/all_gather | solution.py:53
  34.8 7.3 %copy-start.3 = (s32[160]{0:T(256)S(1)}, s32[160]{0:T(256)}, u32[]{:S(2)}) copy-start(s32[160]{0:T(256)} %param.12) | copy-start | bytes 1924
  34.8 99.8 %all-to-all-start.1 = ((bf16[8,128,1024]{2,1,0:T(8,128)(2,1)}), bf16[8,128,1024]{2,1,0:T(8,128)(2,1)}, u32[]{:S(2)}, u32[]{:S(2)}) async-start(bf16[8,128,1024]{2,1,0:T(8,128)(2,1)} %all_to_all.32), calls=%async_computation.1 | async-start | bytes 4194304 | tf_op jit(solution)/shard_map/all_to_all | solution.py:64
  47.6 6.9 %copy-start.4 = (s32[160]{0:T(256)S(1)}, s32[160]{0:T(256)}, u32[]{:S(2)}) copy-start(s32[160]{0:T(256)} %param.14) | copy-start | bytes 1924
  100.4 40.1 %copy-start.2 = (s32[16,256]{1,0:T(8,128)S(1)}, s32[16,256]{1,0:T(8,128)}, u32[]{:S(2)}) copy-start(s32[16,256]{1,0:T(8,128)} %param.18) | copy-start | bytes 49156
  100.4 40.2 %copy-start = (bf16[32,1024]{1,0:T(8,128)(2,1)S(1)}, bf16[32,1024]{1,0:T(8,128)(2,1)}, u32[]{:S(2)}) copy-start(bf16[32,1024]{1,0:T(8,128)(2,1)} %param.17) | copy-start | bytes 196612
  134.5 151.2 %all-to-all-start = ((bf16[1024,8,256]{0,2,1:T(8,128)(2,1)}), bf16[1024,8,256]{0,2,1:T(8,128)(2,1)}, u32[]{:S(2)}, u32[]{:S(2)}) async-start(bf16[1024,8,256]{0,2,1:T(8,128)(2,1)} %all_to_all.28), calls=%async_computation | async-start | bytes 8388608 | tf_op jit(solution)/shard_map/all_to_all | solution.py:49
  140.4 324.5 %reduce-scatter.2.cloned.1.call-start = ((), (), s32[]{:S(2)}) async-start(), calls=%async_computation.4 | async-start | bytes 589824 | tf_op jit(solution)/shard_map/reduce_scatter | solution.py:94
  292.2 15.7 %copy-start.1 = (f32[16,256]{1,0:T(8,128)S(1)}, f32[16,256]{1,0:T(8,128)}, u32[]{:S(2)}) copy-start(f32[16,256]{1,0:T(8,128)} %param.19) | copy-start | bytes 49156
Sparse Core Ops, SparseCore 0:
  9.5 226.6 all-gather.1
  403.9 60.9 reduce-scatter.1
where the time goes:
time: 474 us; the launch traced here: 472 us
  blocking collectives  216 us (46%)
  local copies, waits for them, and re-layouts  107 us (23%)
  waiting for transfers between devices  96 us (20%)
  matrix products  15.2 us (3%)
  between operations  13.6 us (3%)
  starting transfers between devices  13.2 us (3%)
  other arithmetic  10.7 us (2%)
    all_gather x1, blocking collectives, per_device(): full_sketch = lax.all_gather(sketch, 'fsdp', axis=1, tiled=True)  142 us
    psum x1, blocking collectives, per_device(): sketch_rows = lax.psum(partial_sketch, 'fsdp').astype(jnp.bfloat16)  70.7 us
    reduce_scatter x1, waiting for transfers between devices, per_device(): return lax.psum_scatter(products, 'fsdp', scatter_dimension=1, tiled=True)  61.1 us
    all_to_all x1, waiting for transfers between devices, per_device(): lax.all_to_all(down_dense, 'fsdp', split_axis=0, concat_axis=1, tiled=True)  34.2 us
    all_to_all x2, local copies, waits for them, and re-layouts, per_device(): lax.all_to_all(stacked, 'fsdp', split_axis=1, concat_axis=0, tiled=True)  18.5 us
    gather x1, local copies, waits for them, and re-layouts, per_device(): picked = both_weights[probe_index].astype(jnp.float32)  15.7 us
    reshape x2, local copies, waits for them, and re-layouts, per_device(): unpack(down_blocks, down_slot, cell_total)  14.9 us
    another operation x2, local copies, waits for them, and re-layouts, per_device(): stacked = jnp.stack([gate_dense, up_dense], axis=1)  13.8 us
  transfers between devices with their start and end apart: 4, of which 2 were waited for; matrix products, arithmetic and copies ran while one was open for 20% of the time, Pallas kernels for 0%

commit v1 on v0

--- a/solution.py
+++ b/solution.py
@@ -61,7 +61,19 @@
         col_blocks, block_rows, BLK, BLK
     )
     down_dense = down_dense.transpose(0, 2, 1, 3).reshape(col_blocks * BLK, local_width)
-    down_rows = lax.all_to_all(down_dense, "fsdp", split_axis=0, concat_axis=1, tiled=True)
+    ways, here = (lax.axis_size("fsdp"), lax.axis_index("fsdp"))
+    width = down_dense.shape[0] // ways
+    shape = list(down_dense.shape)
+    shape[0] = width
+    height = shape[1]
+    shape[1] = height * ways
+    full = jnp.zeros(shape, down_dense.dtype)
+    for mask in range(ways):
+        part = lax.dynamic_slice_in_dim(down_dense, (here ^ mask) * width, width, axis=0)
+        if mask:
+            part = lax.ppermute(part, "fsdp", [(d, d ^ mask) for d in range(ways)])
+        full = lax.dynamic_update_slice_in_dim(full, part, (here ^ mask) * height, axis=1)
+    down_rows = full
     full_sketch = lax.all_gather(sketch, "fsdp", axis=1, tiled=True)
     projected = contract_last(down_rows, full_sketch)
     projected = projected.astype(jnp.bfloat16)

time: 474 us -> 480 us (1.013)
  waiting for transfers between devices: 96 us -> 67.9 us
  blocking collectives: 216 us -> 242 us
    all_to_all x1 -> x0, waiting for transfers between devices: 34.2 us -> none  [per_device(): lax.all_to_all(down_dense, 'fsdp', split_axis=0, concat_axis=1, tiled=True)]
    all_gather x1, blocking collectives: 142 us -> 161 us  [per_device(): full_sketch = lax.all_gather(sketch, 'fsdp', axis=1, tiled=True)]
    all_to_all x2 -> x0, local copies, waits for them, and re-layouts: 9.57 us -> none  [per_device(): lax.all_to_all(down_dense, 'fsdp', split_axis=0, concat_axis=1, tiled=True)]
    ppermute x0 -> x7, starting transfers between devices: none -> 8.98 us  [per_device(): part = lax.ppermute(part, 'fsdp', [(d, d ^ mask) for d in range(ways)])]
    all_to_all x1 -> x0, starting transfers between devices: 7.26 us -> none  [per_device(): lax.all_to_all(down_dense, 'fsdp', split_axis=0, concat_axis=1, tiled=True)]
    psum x1, blocking collectives: 70.7 us -> 77.4 us  [per_device(): sketch_rows = lax.psum(partial_sketch, 'fsdp').astype(jnp.bfloat16)]
    reshape x0 -> x1, local copies, waits for them, and re-layouts: none -> 5.47 us  [per_device(): down_dense.transpose(0, 2, 1, 3).reshape(col_blocks * BLK, local_width)]
    dynamic_update_slice x0 -> x7, local copies, waits for them, and re-layouts: none -> 5.16 us  [per_device(): lax.dynamic_update_slice_in_dim(full, part, (here ^ mask) * height, axis=1)]
  transfers between devices with their start and end apart: 4 -> 10, of which waited for: 2 -> 3; matrix products, arithmetic and copies ran while one was open for 20% -> 22% of each run, Pallas kernels for 0% -> 0%
where the time goes in v1:
time: 480 us; the launch traced here: 478 us
  blocking collectives  242 us (50%)
  local copies, waits for them, and re-layouts  110 us (23%)
  waiting for transfers between devices  67.9 us (14%)
  matrix products  17.2 us (4%)
  starting transfers between devices  16.6 us (3%)
  between operations  13.8 us (3%)
  other arithmetic  10.7 us (2%)
    all_gather x1, blocking collectives, per_device(): full_sketch = lax.all_gather(sketch, 'fsdp', axis=1, tiled=True)  161 us
    psum x1, blocking collectives, per_device(): sketch_rows = lax.psum(partial_sketch, 'fsdp').astype(jnp.bfloat16)  77.4 us
    reduce_scatter x1, waiting for transfers between devices, per_device(): return lax.psum_scatter(products, 'fsdp', scatter_dimension=1, tiled=True)  62.2 us
    all_to_all x2, local copies, waits for them, and re-layouts, per_device(): lax.all_to_all(stacked, 'fsdp', split_axis=1, concat_axis=0, tiled=True)  18.5 us
    gather x1, local copies, waits for them, and re-layouts, per_device(): picked = both_weights[probe_index].astype(jnp.float32)  15.7 us
    reshape x2, local copies, waits for them, and re-layouts, per_device(): unpack(down_blocks, down_slot, cell_total)  14.5 us
    another operation x2, local copies, waits for them, and re-layouts, per_device(): stacked = jnp.stack([gate_dense, up_dense], axis=1)  13.8 us
    transpose x1, local copies, waits for them, and re-layouts, per_device(): stacked.transpose(0, 4, 2, 1, 3, 5)  13.1 us
  transfers between devices with their start and end apart: 10, of which 3 were waited for; matrix products, arithmetic and copies ran while one was open for 22% of the time, Pallas kernels for 0%

profile of v1, /device:TPU:0, one launch (start us, length us, event | category | flops | bytes accessed | tf_op | source)
XLA Modules:
  0.0 478.2 jit_solution(10256307978967145144)
XLA Ops:
  6.5 0.7 all-gather.2.cloned.1.call-update
  7.3 0.7 compare_select_fusion.1
  8.0 3.9 scatter_custom_fusion.1
  11.8 1.5 slice.31
  13.3 6.9 %stack.8 = bf16[16,1,8,2,64,64]{5,4,3,2,0,1:T(8,128)(2,1)} reshape(bf16[256,4096]{1,0:T(8,128)(2,1)} %slice.31) | data formatting | bytes 4194304 | tf_op jit(solution)/shard_map/stack | solution.py:46
  20.2 3.9 scatter_custom_fusion
  24.2 1.5 slice.30
  25.7 6.9 %stack.7 = bf16[16,1,8,2,64,64]{5,4,3,2,0,1:T(8,128)(2,1)} reshape(bf16[256,4096]{1,0:T(8,128)(2,1)} %slice.30) | data formatting | bytes 4194304 | tf_op jit(solution)/shard_map/stack | solution.py:46
  32.6 8.6 %maximum_bitcast_fusion = bf16[16,64,8,2,2,64]{5,1,4,2,0,3:T(8,128)(2,1)} fusion(bf16[16,1,8,2,64,64]{5,4,3,2,0,1:T(8,128)(2,1)} %stack.8, bf16[16,1,8,2,64,64]{5,4,3,2,0,1:T(8,128)(2,1)} %stack.7), kind=kLoop, calls=%fused_computation.4 | loop fusion | flops 2097152 | bytes 8388608 | tf_op jit(solution)/shard_map/transpose | solution.py:48
  41.2 13.1 %copy.19 = bf16[16,64,8,2,2,64]{1,0,5,4,3,2:T(8,128)(2,1)} copy(bf16[16,64,8,2,2,64]{5,1,4,2,0,3:T(8,128)(2,1)} %maximum_bitcast_fusion) | data formatting | bytes 8388608 | tf_op jit(solution)/shard_map/transpose | solution.py:48
  54.3 12.0 %all_to_all.14 = bf16[1024,8,256]{0,2,1:T(8,128)(2,1)} reshape(bf16[16,64,8,2,2,64]{1,0,5,4,3,2:T(8,128)(2,1)} %copy.19) | data formatting | bytes 8388608 | tf_op jit(solution)/shard_map/all_to_all | solution.py:49
  66.3 7.6 %all-to-all-start = ((bf16[1024,8,256]{0,2,1:T(8,128)(2,1)}), bf16[1024,8,256]{0,2,1:T(8,128)(2,1)}, u32[]{:S(2)}, u32[]{:S(2)}) async-start(bf16[1024,8,256]{0,2,1:T(8,128)(2,1)} %all_to_all.14), calls=%async_computation | async-start | bytes 8388608 | tf_op jit(solution)/shard_map/all_to_all | solution.py:49
  73.9 3.9 scatter_custom_fusion.2
  77.8 1.5 slice.36
  79.2 6.9 %reshape.37 = bf16[16,16,64,64]{3,2,1,0:T(8,128)(2,1)} reshape(bf16[256,4096]{1,0:T(8,128)(2,1)} %slice.36) | data formatting | bytes 4194304 | tf_op jit(solution)/shard_map/reshape | solution.py:60
  86.1 7.7 %copy.30 = bf16[16,16,64,64]{3,1,2,0:T(8,128)(2,1)} copy(bf16[16,16,64,64]{3,2,1,0:T(8,128)(2,1)} %reshape.37) | data formatting | bytes 4194304 | tf_op jit(solution)/shard_map/reshape | solution.py:60
  93.8 5.5 %reshape.38 = bf16[1024,1024]{1,0:T(8,128)(2,1)S(1)} reshape(bf16[16,64,16,64]{3,2,1,0:T(8,128)(2,1)} %bitcast.40) | data formatting | bytes 4194304 | tf_op jit(solution)/shard_map/reshape | solution.py:63
  99.5 1.0 constant_dynamic-slice_fusion
  100.5 1.3 copy-done
  101.9 1.9 collective-permute-start
  103.8 1.5 collective-permute-start.1
  105.4 2.8 collective-permute-start.3
  108.2 1.5 collective-permute-start.4
  109.7 161.0 %all_gather.7 = bf16[32,8192]{1,0:T(8,128)(2,1)S(1)} all-gather(bf16[32,1024]{1,0:T(8,128)(2,1)S(1)} %copy-done.1), channel_id=1, replica_groups=mesh['groups'=2,'fsdp'=8,'seq'=2] {'fsdp'}, dimensions={1}, use_global_device_ids=true | all-gather | bytes 589824 | tf_op jit(solution)/shard_map/all_gather | solution.py:77
  270.8 0.6 collective-permute-start.5
  271.4 0.8 constant_dynamic-update-slice_fusion.5
  272.1 0.6 collective-permute-start.6
  272.7 0.7 constant_dynamic-update-slice_fusion.4
  273.4 0.8 constant_dynamic-update-slice_fusion.3
  274.2 0.7 constant_dynamic-update-slice_fusion.2
  274.9 0.7 constant_dynamic-update-slice_fusion.1
  275.7 3.3 collective-permute-done.5
  279.0 0.8 constant_dynamic-update-slice_fusion
  279.8 1.5 collective-permute-done.6
  281.3 0.7 constant_dynamic-update-slice_fusion.6
  282.0 2.4 convolution_convert_fusion
  284.4 6.5 %copy.20 = bf16[8,1024,256]{2,1,0:T(8,128)(2,1)} copy(bf16[8,1024,256]{1,2,0:T(8,128)(2,1)} %bitcast.1) | data formatting | bytes 8388608 | tf_op jit(solution)/shard_map/all_to_all | solution.py:49
  290.9 15.7 %gather_fusion = bf16[4096,256]{1,0:T(8,128)(2,1)S(1)} fusion(bf16[8192,256]{1,0:T(8,128)(2,1)} %bitcast.37, s32[4096]{0:T(1024)S(1)} %broadcast_clamp_fusion), kind=kCustom, calls=%fused_computation | custom fusion | bytes 4210688 | tf_op jit(solution)/shard_map/gather | solution.py:50
  306.7 0.7 fusion
  307.4 7.0 %convolution_bitcast_fusion = f32[512,256]{0,1:T(8,128)S(1)} fusion(bf16[8192,256]{1,0:T(8,128)(2,1)} %bitcast.38, bf16[512,8192]{1,0:T(8,128)(2,1)} %all-gather.2.cloned.1.call-done), kind=kOutput, calls=%fused_computation.11 | convolution fusion | flops 2147483648 | bytes 13107200 | tf_op jit(solution)/shard_map/dot_general | solution.py:52
  315.4 1.4 copy.23
  316.8 2.6 fusion.14
  319.4 3.5 reshape.39
  323.0 77.4 %all-reduce.1 = bf16[512,512]{1,0:T(8,128)(2,1)S(1)} all-reduce(f32[512,512]{1,0:T(8,128)S(1)} %reshape.39), channel_id=1, replica_groups=mesh['groups'=2,'fsdp'=8,'seq'=2] {'fsdp'}, use_global_device_ids=true, to_apply=%region_4.0 | all-reduce | flops 262144 | bytes 1572864 | tf_op jit(solution)/shard_map/psum | solution.py:93
  400.6 1.0 multiply_reduce_fusion.1
  401.6 3.4 psum.15
  404.9 4.2 fusion.15
  409.1 62.2 %reduce-scatter.2.cloned.1.call-done = f32[16,1024]{1,0:T(8,128)} async-done(((f32[16,8192]{1,0:T(8,128)}), f32[16,1024]{1,0:T(8,128)}) %reduce-scatter.2.cloned.1.call-update) | async-done | bytes 65552 | tf_op jit(solution)/shard_map/reduce_scatter | solution.py:106
  (32 shorter events, 1.6 us)
Async XLA Ops:
  6.5 300.9 %all-gather.2.cloned.1.call-start = ((), (), s32[]{:S(2)}) async-start(), calls=%async_computation.2 | async-start | bytes 9437184 | tf_op jit(solution)/shard_map/all_gather | solution.py:53
  13.3 6.9 %copy-start.4 = (s32[160]{0:T(256)S(1)}, s32[160]{0:T(256)}, u32[]{:S(2)}) copy-start(s32[160]{0:T(256)} %param.12) | copy-start | bytes 1924
  66.3 218.2 %all-to-all-start = ((bf16[1024,8,256]{0,2,1:T(8,128)(2,1)}), bf16[1024,8,256]{0,2,1:T(8,128)(2,1)}, u32[]{:S(2)}, u32[]{:S(2)}) async-start(bf16[1024,8,256]{0,2,1:T(8,128)(2,1)} %all_to_all.14), calls=%async_computation | async-start | bytes 8388608 | tf_op jit(solution)/shard_map/all_to_all | solution.py:49
  73.8 397.5 %reduce-scatter.2.cloned.1.call-start = ((), (), s32[]{:S(2)}) async-start(), calls=%async_computation.3 | async-start | bytes 589824 | tf_op jit(solution)/shard_map/reduce_scatter | solution.py:106
  99.5 10.2 %copy-start.1 = (bf16[32,1024]{1,0:T(8,128)(2,1)S(1)}, bf16[32,1024]{1,0:T(8,128)(2,1)}, u32[]{:S(2)}) copy-start(bf16[32,1024]{1,0:T(8,128)(2,1)} %param.17) | copy-start | bytes 196612
  99.5 171.2 %copy-start.3 = (s32[16,256]{1,0:T(8,128)S(1)}, s32[16,256]{1,0:T(8,128)}, u32[]{:S(2)}) copy-start(s32[16,256]{1,0:T(8,128)} %param.18) | copy-start | bytes 49156
  100.5 1.3 copy-start
  101.9 168.9 %collective-permute-start = (bf16[128,1024]{1,0:T(8,128)(2,1)}, bf16[128,1024]{1,0:T(8,128)(2,1)S(1)}, u32[]{:S(2)}, u32[]{:S(2)}) collective-permute-start(bf16[128,1024]{1,0:T(8,128)(2,1)} %get-tuple-element.13), channel_id=1, source_target_pairs={{0,2},{2,0},{4,6},{6,4},{8,10},{10,8},{12,14},{14,12},{1,3},{3,1},... | collective-permute-start | bytes 786440 | tf_op jit(solution)/shard_map/ppermute | solution.py:74
  103.8 168.3 %collective-permute-start.1 = (bf16[128,1024]{1,0:T(8,128)(2,1)}, bf16[128,1024]{1,0:T(8,128)(2,1)S(1)}, u32[]{:S(2)}, u32[]{:S(2)}) collective-permute-start(bf16[128,1024]{1,0:T(8,128)(2,1)} %get-tuple-element.12), channel_id=1, source_target_pairs={{0,4},{2,6},{4,0},{6,2},{8,12},{10,14},{12,8},{14,10},{1,5},{3,7},... | collective-permute-start | bytes 786440 | tf_op jit(solution)/shard_map/ppermute | solution.py:74
  105.3 168.2 %collective-permute-start.2 = (bf16[128,1024]{1,0:T(8,128)(2,1)S(1)}, bf16[128,1024]{1,0:T(8,128)(2,1)S(1)}, u32[]{:S(2)}, u32[]{:S(2)}) collective-permute-start(bf16[128,1024]{1,0:T(8,128)(2,1)S(1)} %get-tuple-element.11), channel_id=1, source_target_pairs={{0,6},{2,4},{4,2},{6,0},{8,14},{10,12},{12,10},{14,8},{1,7},{3,5},... | collective-permute-start | bytes 786440 | tf_op jit(solution)/shard_map/ppermute | solution.py:74
  105.4 168.8 %collective-permute-start.3 = (bf16[128,1024]{1,0:T(8,128)(2,1)S(1)}, bf16[128,1024]{1,0:T(8,128)(2,1)S(1)}, u32[]{:S(2)}, u32[]{:S(2)}) collective-permute-start(bf16[128,1024]{1,0:T(8,128)(2,1)S(1)} %get-tuple-element.10), channel_id=1, source_target_pairs={{0,8},{2,10},{4,12},{6,14},{8,0},{10,2},{12,4},{14,6},{1,9},{3,11}... | collective-permute-start | bytes 786440 | tf_op jit(solution)/shard_map/ppermute | solution.py:74
  108.2 166.7 %collective-permute-start.4 = (bf16[128,1024]{1,0:T(8,128)(2,1)S(1)}, bf16[128,1024]{1,0:T(8,128)(2,1)S(1)}, u32[]{:S(2)}, u32[]{:S(2)}) collective-permute-start(bf16[128,1024]{1,0:T(8,128)(2,1)S(1)} %get-tuple-element.9), channel_id=1, source_target_pairs={{0,10},{2,8},{4,14},{6,12},{8,2},{10,0},{12,6},{14,4},{1,11},{3,9}... | collective-permute-start | bytes 786440 | tf_op jit(solution)/shard_map/ppermute | solution.py:74
  270.8 8.2 %collective-permute-start.5 = (bf16[128,1024]{1,0:T(8,128)(2,1)S(1)}, bf16[128,1024]{1,0:T(8,128)(2,1)S(1)}, u32[]{:S(2)}, u32[]{:S(2)}) collective-permute-start(bf16[128,1024]{1,0:T(8,128)(2,1)S(1)} %get-tuple-element.8), channel_id=1, source_target_pairs={{0,12},{2,14},{4,8},{6,10},{8,4},{10,6},{12,0},{14,2},{1,13},{3,15... | collective-permute-start | bytes 786440 | tf_op jit(solution)/shard_map/ppermute | solution.py:74
  272.1 9.2 %collective-permute-start.6 = (bf16[128,1024]{1,0:T(8,128)(2,1)S(1)}, bf16[128,1024]{1,0:T(8,128)(2,1)S(1)}, u32[]{:S(2)}, u32[]{:S(2)}) collective-permute-start(bf16[128,1024]{1,0:T(8,128)(2,1)S(1)} %get-tuple-element.7), channel_id=1, source_target_pairs={{0,14},{2,12},{4,10},{6,8},{8,6},{10,4},{12,2},{14,0},{1,15},{3,13... | collective-permute-start | bytes 786440 | tf_op jit(solution)/shard_map/ppermute | solution.py:74
  290.9 15.7 %copy-start.2 = (f32[16,256]{1,0:T(8,128)S(1)}, f32[16,256]{1,0:T(8,128)}, u32[]{:S(2)}) copy-start(f32[16,256]{1,0:T(8,128)} %param.19) | copy-start | bytes 49156
Sparse Core Ops, SparseCore 0:
  9.5 201.5 all-gather.1
  409.3 62.0 reduce-scatter.1
